TPU v7x, 32 devices: a whole 2x2x4 slice. The times are simulated.
32 devices in a mesh: rad: 8 (over z, y), ell: 4 (over x, core).
Axes of the slice: x: 2, y: 2, z: 4, core: 2. Of those that a mesh axis runs over, the one named last changes fastest.
Arguments:
- field: bfloat16 [512, 128, 512], P('rad', 'ell'), may hold values from -6 to 6
- projection: bfloat16 [512, 128, 256], P('rad', 'ell'), may hold values from -0.375 to 0.375
- ell_ids: int32 [128], P('ell'), may hold values from 0 to 255, as said below
Outputs:
- share: float32 [128, 256], P('ell', 'rad')
- crest: float32 [128, 256], P('ell', 'rad')
Inputs may be any that keep to these rules, and one draw needn't show every extreme that they name: `ell_ids`: distinct and ascending.
All inputs are finite; a program needn't handle non-finite values.
Results may differ from a plain program's by a relative error of at most 0.0003.
Values may be sent and summed in bfloat16 or wider, within the bound.
A program may use at most 64 MiB of HBM per device.

v0:
```python
import jax
import jax.numpy as jnp
from jax import lax
from jax.sharding import PartitionSpec as P


def per_device(field, projection, ell_ids):
    exchanged = lax.all_to_all(field, "rad", split_axis=2, concat_axis=0, tiled=True)
    slot_share = exchanged.shape[2]
    coef = jnp.einsum(
        "rem,ren->emn",
        exchanged,
        lax.all_gather(projection, "rad", axis=0, tiled=True),
        preferred_element_type=jnp.float32,
    )
    slots = lax.axis_index("rad") * slot_share + jnp.arange(slot_share, dtype=jnp.int32)
    valid = (slots[None, :] < 2 * ell_ids[:, None] + 1).astype(jnp.float32)
    energy_part = jnp.sum(valid[:, :, None] * coef * coef, axis=1)
    peak_part = jnp.max(valid[:, :, None] * jnp.abs(coef), axis=1)
    energy_all, peak_all = (
        lax.all_to_all(energy_part[None], "rad", split_axis=2, concat_axis=0, tiled=True),
        lax.all_to_all(peak_part[None], "rad", split_axis=2, concat_axis=0, tiled=True),
    )
    energy = jnp.sum(energy_all, axis=0)
    peak = jnp.max(peak_all, axis=0)
    local_sum = jnp.sum(energy, axis=0)
    local_top = jnp.max(peak, axis=0)
    column = lax.psum(local_sum, "ell")
    top = lax.pmax(local_top, "ell")
    column = column + 1e-06
    top = top + 1e-06
    total_ells = ell_ids.shape[0] * lax.axis_size("ell")
    share = total_ells * energy / column[None, :]
    crest = peak / top[None, :]
    return (share, crest)


def solution(mesh):
    in_specs = (P("rad", "ell", None), P("rad", "ell", None), P("ell"))
    out_specs = (P("ell", "rad"), P("ell", "rad"))
    return jax.shard_map(
        per_device, mesh=mesh, in_specs=in_specs, out_specs=out_specs, check_vma=False
    )
```

profile of v0, /device:TPU:0, one launch (start us, length us, event | category | flops | bytes accessed | tf_op | source)
XLA Modules:
  0.0 218.3 jit_solution(14163633866488096663)
XLA Ops:
  7.2 2.9 %copy.19 = bf16[64,32,256]{2,0,1:T(8,128)(2,1)} copy(bf16[64,32,256]{2,1,0:T(8,128)(2,1)} %param.4) | data formatting | bytes 2097152 | tf_op args[1]
  10.2 7.8 %copy.17 = bf16[64,32,512]{0,1,2:T(8,128)(2,1)} copy(bf16[64,32,512]{2,1,0:T(8,128)(2,1)S(1)} %copy-done) | data formatting | bytes 4194304 | tf_op args[0]
  18.0 7.7 %reshape.45 = bf16[8,2,65536]{2,1,0:T(2,128)(2,1)} reshape(bf16[512,32,64]{2,1,0:T(8,128)(2,1)} %bitcast.22) | data formatting | bytes 4194304
  25.7 7.5 %all-to-all-start = ((bf16[8,2,65536]{2,1,0:T(2,128)(2,1)}), bf16[8,2,65536]{2,1,0:T(2,128)(2,1)S(1)}, u32[]{:S(2)}, u32[]{:S(2)}) async-start(bf16[8,2,65536]{2,1,0:T(2,128)(2,1)} %reshape.45), calls=%async_computation | async-start | bytes 4194304 | tf_op jit(solution)/shard_map/all_to_all | solution.py:8
  33.2 87.4 %all-to-all-done = bf16[8,2,65536]{2,1,0:T(2,128)(2,1)S(1)} async-done(((bf16[8,2,65536]{2,1,0:T(2,128)(2,1)}), bf16[8,2,65536]{2,1,0:T(2,128)(2,1)S(1)}, u32[]{:S(2)}, u32[]{:S(2)}) %all-to-all-start) | async-done | bytes 2097184 | tf_op jit(solution)/shard_map/all_to_all | solution.py:8
  120.7 5.0 %reshape.46 = bf16[512,32,64]{2,1,0:T(8,128)(2,1)} reshape(bf16[8,2,65536]{2,1,0:T(2,128)(2,1)S(1)} %all-to-all-done) | data formatting | bytes 4194304
  125.7 6.8 %copy.25 = bf16[64,32,8,64]{0,2,3,1:T(8,128)(2,1)} copy(bf16[64,32,8,64]{0,1,3,2:T(8,128)(2,1)} %bitcast.23) | data formatting | bytes 4194304 | tf_op jit(solution)/shard_map/all_to_all | solution.py:8
  132.5 5.4 %all_to_all.34 = bf16[512,32,64]{0,2,1:T(8,128)(2,1)S(1)} reshape(bf16[8,64,32,64]{1,0,3,2:T(8,128)(2,1)} %bitcast.24) | data formatting | bytes 4194304 | tf_op jit(solution)/shard_map/all_to_all | solution.py:8
  137.9 35.0 %all-gather.2.cloned.1.call-done = bf16[512,32,256]{2,0,1:T(8,128)(2,1)} async-done(((bf16[64,32,256]{2,0,1:T(8,128)(2,1)}), bf16[512,32,256]{2,0,1:T(8,128)(2,1)}) %all-gather.2.cloned.1.call-update) | async-done | bytes 8388624 | tf_op jit(solution)/shard_map/all_gather | solution.py:13
  172.9 4.9 %multiply_reduce_fusion = (f32[32,256]{1,0:T(8,128)S(1)}, f32[32,256]{1,0:T(8,128)S(1)}) fusion(f32[32,64]{1,0:T(8,128)S(1)} %compare_convert_fusion, bf16[512,32,64]{0,2,1:T(8,128)(2,1)S(1)} %all_to_all.34, bf16[512,32,256]{2,0,1:T(8,128)(2,1)} %all-gather.2.cloned.1.call-done), kind=kOutput, calls=%fused_computation.3 | convolution fusion | flops 540000256 | bytes 10559488 | tf_op jit(solution)/shard_map/rem,ren->emn/dot_general | solution.py:10
  178.4 1.0 reduce.18
  179.4 0.7 reshape.49
  180.1 3.3 %all-to-all-start.2 = ((f32[8,1,1024]{2,1,0:T(1,128)}), f32[8,1,1024]{2,1,0:T(1,128)S(1)}, u32[]{:S(2)}, u32[]{:S(2)}) async-start(f32[8,1,1024]{2,1,0:T(1,128)} %reshape.49), calls=%async_computation.2 | async-start | bytes 65536 | tf_op jit(solution)/shard_map/all_to_all | solution.py:22
  183.6 1.0 reduce.16
  184.6 0.7 reshape.47
  185.3 4.8 %all-to-all-done.2 = f32[8,1,1024]{2,1,0:T(1,128)S(1)} async-done(((f32[8,1,1024]{2,1,0:T(1,128)}), f32[8,1,1024]{2,1,0:T(1,128)S(1)}, u32[]{:S(2)}, u32[]{:S(2)}) %all-to-all-start.2) | async-done | bytes 32800 | tf_op jit(solution)/shard_map/all_to_all | solution.py:22
  190.1 3.3 %all-to-all-start.1 = ((f32[8,1,1024]{2,1,0:T(1,128)}), f32[8,1,1024]{2,1,0:T(1,128)S(1)}, u32[]{:S(2)}, u32[]{:S(2)}) async-start(f32[8,1,1024]{2,1,0:T(1,128)} %reshape.47), calls=%async_computation.1 | async-start | bytes 65536 | tf_op jit(solution)/shard_map/all_to_all | solution.py:21
  193.4 0.7 reduce.19
  194.4 1.0 bitcast_reduce_fusion
  195.6 6.0 %pmax.7 = f32[32]{0:T(128)S(1)} all-reduce(f32[32]{0:T(128)S(1)} %reduce_max.38), channel_id=1, replica_groups=mesh['rad'=8,'ell'=4] {'ell'}, use_global_device_ids=true, to_apply=%region_9.10 | all-reduce | flops 32 | bytes 256 | tf_op jit(solution)/shard_map/pmax | solution.py:29
  201.6 0.7 copy.23
  202.3 0.7 reduce.17
  203.2 1.0 bitcast_reduce_fusion.1
  204.4 6.3 %psum.7 = f32[32]{0:T(128)S(1)} all-reduce(f32[32]{0:T(128)S(1)} %reduce_sum.38), channel_id=1, replica_groups=mesh['rad'=8,'ell'=4] {'ell'}, use_global_device_ids=true, to_apply=%region_4.0 | all-reduce | flops 32 | bytes 256 | tf_op jit(solution)/shard_map/psum | solution.py:28
  (26 shorter events, 2.4 us)
Async XLA Ops:
  7.2 3.0 %copy-start = (bf16[64,32,512]{2,1,0:T(8,128)(2,1)S(1)}, bf16[64,32,512]{2,1,0:T(8,128)(2,1)}, u32[]{:S(2)}) copy-start(bf16[64,32,512]{2,1,0:T(8,128)(2,1)} %param.3) | copy-start | bytes 6291460
  7.2 165.7 %all-gather.2.cloned.1.call-start = ((), (), s32[]{:S(2)}) async-start(), calls=%async_computation.3 | async-start | bytes 9437184 | tf_op jit(solution)/shard_map/all_gather | solution.py:13
  25.7 7.5 %copy-start.1 = (s32[32]{0:T(128)S(1)}, s32[32]{0:T(128)}, u32[]{:S(2)}) copy-start(s32[32]{0:T(128)} %param.5) | copy-start | bytes 388
  25.7 95.0 %all-to-all-start = ((bf16[8,2,65536]{2,1,0:T(2,128)(2,1)}), bf16[8,2,65536]{2,1,0:T(2,128)(2,1)S(1)}, u32[]{:S(2)}, u32[]{:S(2)}) async-start(bf16[8,2,65536]{2,1,0:T(2,128)(2,1)} %reshape.45), calls=%async_computation | async-start | bytes 4194304 | tf_op jit(solution)/shard_map/all_to_all | solution.py:8
  180.1 10.0 %all-to-all-start.2 = ((f32[8,1,1024]{2,1,0:T(1,128)}), f32[8,1,1024]{2,1,0:T(1,128)S(1)}, u32[]{:S(2)}, u32[]{:S(2)}) async-start(f32[8,1,1024]{2,1,0:T(1,128)} %reshape.49), calls=%async_computation.2 | async-start | bytes 65536 | tf_op jit(solution)/shard_map/all_to_all | solution.py:22
  190.1 12.2 %all-to-all-start.1 = ((f32[8,1,1024]{2,1,0:T(1,128)}), f32[8,1,1024]{2,1,0:T(1,128)S(1)}, u32[]{:S(2)}, u32[]{:S(2)}) async-start(f32[8,1,1024]{2,1,0:T(1,128)} %reshape.47), calls=%async_computation.1 | async-start | bytes 65536 | tf_op jit(solution)/shard_map/all_to_all | solution.py:21
Sparse Core Ops, SparseCore 0:
  10.3 162.5 all-gather.1
where the time goes:
time: 219 us; the launch traced here: 218 us
  waiting for transfers between devices  127 us (58%)
  local copies, waits for them, and re-layouts  39.8 us (18%)
  starting transfers between devices  14.2 us (6%)
  between operations  14.2 us (6%)
  blocking collectives  12.3 us (6%)
  other arithmetic  5.77 us (3%)
  matrix products  4.92 us (2%)
    all_to_all x1, waiting for transfers between devices, per_device(): lax.all_to_all(field, 'rad', split_axis=2, concat_axis=0, tiled=True)  87.4 us
    all_gather x1, waiting for transfers between devices, per_device(): lax.all_gather(projection, 'rad', axis=0, tiled=True)  35 us
    unnamed x15, local copies, waits for them, and re-layouts  27.2 us
    all_to_all x2, local copies, waits for them, and re-layouts, per_device(): lax.all_to_all(field, 'rad', split_axis=2, concat_axis=0, tiled=True)  12.2 us
    all_to_all x1, starting transfers between devices, per_device(): lax.all_to_all(field, 'rad', split_axis=2, concat_axis=0, tiled=True)  7.47 us
    psum x1, blocking collectives, per_device(): column = lax.psum(local_sum, 'ell')  6.3 us
    pmax x1, blocking collectives, per_device(): top = lax.pmax(local_top, 'ell')  5.96 us
    dot_general x1, matrix products, per_device(): jnp.einsum('rem,ren->emn', exchanged, lax.all_gather(projection, 'rad', a...  4.92 us
  transfers between devices with their start and end apart: 4, of which 3 were waited for; matrix products, arithmetic and copies ran while one was open for 15% of the time, Pallas kernels for 0%

commit v1 on v0

--- a/solution.py
+++ b/solution.py
@@ -7,12 +7,37 @@
 def per_device(field, projection, ell_ids):
     exchanged = lax.all_to_all(field, "rad", split_axis=2, concat_axis=0, tiled=True)
     slot_share = exchanged.shape[2]
+    peers, here, rows = (lax.axis_size("rad"), lax.axis_index("rad"), projection.shape[0])
+    upward = [(i, (i + 1) % peers) for i in range(peers)]
+    behind = [(i, (i - 1) % peers) for i in range(peers)]
+    half = peers // 2
+    from_left = from_right = projection
     coef = jnp.einsum(
         "rem,ren->emn",
-        exchanged,
-        lax.all_gather(projection, "rad", axis=0, tiled=True),
+        lax.dynamic_slice_in_dim(exchanged, here * rows, projection.shape[0], axis=0),
+        projection,
         preferred_element_type=jnp.float32,
     )
+    for step in range(1, half + 1):
+        from_left = lax.ppermute(from_left, "rad", upward)
+        if step < peers - half:
+            from_right = lax.ppermute(from_right, "rad", behind)
+            coef = coef + jnp.einsum(
+                "rem,ren->emn",
+                lax.dynamic_slice_in_dim(
+                    exchanged, (here + step) % peers * rows, from_right.shape[0], axis=0
+                ),
+                from_right,
+                preferred_element_type=jnp.float32,
+            )
+        coef = coef + jnp.einsum(
+            "rem,ren->emn",
+            lax.dynamic_slice_in_dim(
+                exchanged, (here - step) % peers * rows, from_left.shape[0], axis=0
+            ),
+            from_left,
+            preferred_element_type=jnp.float32,
+        )
     slots = lax.axis_index("rad") * slot_share + jnp.arange(slot_share, dtype=jnp.int32)
     valid = (slots[None, :] < 2 * ell_ids[:, None] + 1).astype(jnp.float32)
     energy_part = jnp.sum(valid[:, :, None] * coef * coef, axis=1)

time: 219 us -> 255 us (1.16)
  starting transfers between devices: 14.2 us -> 37.3 us
  waiting for transfers between devices: 127 us -> 147 us
  between operations: 14.2 us -> 0.83 us
  matrix products: 4.92 us -> 13 us
    ppermute x0 -> x7, waiting for transfers between devices: none -> 142 us  [the longest x4 142 us: per_device(): from_left = lax.ppermute(from_left, 'rad', upward)]
    all_to_all x1, waiting for transfers between devices: 87.4 us -> 0.01 us  [per_device(): lax.all_to_all(field, 'rad', split_axis=2, concat_axis=0, tiled=True)]
    all_gather x1 -> x0, waiting for transfers between devices: 35 us -> none  [per_device(): lax.all_gather(projection, 'rad', axis=0, tiled=True)]
    ppermute x0 -> x7, starting transfers between devices: none -> 19.9 us  [the longest x3 10.2 us: per_device(): from_right = lax.ppermute(from_right, 'rad', behind)]
    dot_general x1 -> x8, matrix products: 4.92 us -> 13 us  [the longest x4 6.84 us: per_device(): jnp.einsum('rem,ren->emn', lax.dynamic_slice_in_dim(exchanged, (here - st...]
    all_to_all x1, waiting for transfers between devices: 0.01 us -> 4.89 us  [per_device(): lax.all_to_all(energy_part[None], 'rad', split_axis=2, concat_axis=0, til...]
    all_to_all x1, waiting for transfers between devices: 4.82 us -> 0.01 us  [per_device(): lax.all_to_all(peak_part[None], 'rad', split_axis=2, concat_axis=0, tiled...]
    all_to_all x1, starting transfers between devices: 3.33 us -> 6.65 us  [per_device(): lax.all_to_all(energy_part[None], 'rad', split_axis=2, concat_axis=0, til...]
  transfers between devices with their start and end apart: 4 -> 10, of which waited for: 3 -> 4; matrix products, arithmetic and copies ran while one was open for 15% -> 11% of each run, Pallas kernels for 0% -> 0%
where the time goes in v1:
time: 255 us; the launch traced here: 254 us
  waiting for transfers between devices  147 us (58%)
  local copies, waits for them, and re-layouts  38.3 us (15%)
  starting transfers between devices  37.3 us (15%)
  matrix products  13 us (5%)
  blocking collectives  12.3 us (5%)
  other arithmetic  5.77 us (2%)
    ppermute x4, waiting for transfers between devices, per_device(): from_left = lax.ppermute(from_left, 'rad', upward)  142 us
    unnamed x19, local copies, waits for them, and re-layouts  25.7 us
    all_to_all x2, local copies, waits for them, and re-layouts, per_device(): lax.all_to_all(field, 'rad', split_axis=2, concat_axis=0, tiled=True)  12.2 us
    ppermute x3, starting transfers between devices, per_device(): from_right = lax.ppermute(from_right, 'rad', behind)  10.2 us
    ppermute x4, starting transfers between devices, per_device(): from_left = lax.ppermute(from_left, 'rad', upward)  9.61 us
    all_to_all x1, starting transfers between devices, per_device(): lax.all_to_all(field, 'rad', split_axis=2, concat_axis=0, tiled=True)  7.44 us
    dot_general x4, matrix products, per_device(): jnp.einsum('rem,ren->emn', lax.dynamic_slice_in_dim(exchanged, (here - st...  6.84 us
    all_to_all x1, starting transfers between devices, per_device(): lax.all_to_all(energy_part[None], 'rad', split_axis=2, concat_axis=0, til...  6.65 us
  transfers between devices with their start and end apart: 10, of which 4 were waited for; matrix products, arithmetic and copies ran while one was open for 11% of the time, Pallas kernels for 0%

profile of v1, /device:TPU:0, one launch (start us, length us, event | category | flops | bytes accessed | tf_op | source)
XLA Modules:
  0.0 254.5 jit_solution(3146356647617033237)
XLA Ops:
  0.6 8.8 %copy.23 = bf16[64,32,512]{0,1,2:T(8,128)(2,1)} copy(bf16[64,32,512]{2,1,0:T(8,128)(2,1)} %param.3) | data formatting | bytes 4194304 | tf_op args[0]
  9.4 7.6 %reshape.45 = bf16[8,2,65536]{2,1,0:T(2,128)(2,1)} reshape(bf16[512,32,64]{2,1,0:T(8,128)(2,1)} %bitcast.27) | data formatting | bytes 4194304
  17.0 7.4 %all-to-all-start = ((bf16[8,2,65536]{2,1,0:T(2,128)(2,1)}), bf16[8,2,65536]{2,1,0:T(2,128)(2,1)S(1)}, u32[]{:S(2)}, u32[]{:S(2)}) async-start(bf16[8,2,65536]{2,1,0:T(2,128)(2,1)} %reshape.45), calls=%async_computation | async-start | bytes 4194304 | tf_op jit(solution)/shard_map/all_to_all | solution.py:8
  25.0 2.1 collective-permute-start.1
  27.1 2.8 %collective-permute-start = (bf16[64,32,256]{2,0,1:T(8,128)(2,1)S(1)}, bf16[64,32,256]{2,0,1:T(8,128)(2,1)}, u32[]{:S(2)}, u32[]{:S(2)}) collective-permute-start(bf16[64,32,256]{2,0,1:T(8,128)(2,1)S(1)} %copy.25), channel_id=1, source_target_pairs={{0,28},{4,0},{8,4},{12,8},{16,12},{20,16},{24,20},{28,24},{1,29},{... | collective-permute-start | bytes 3145736 | tf_op jit(solution)/shard_map/ppermute | solution.py:24
  29.8 62.1 %collective-permute-done.1 = bf16[64,32,256]{2,0,1:T(8,128)(2,1)S(1)} collective-permute-done((bf16[64,32,256]{2,0,1:T(8,128)(2,1)S(1)}, bf16[64,32,256]{2,0,1:T(8,128)(2,1)S(1)}, u32[]{:S(2)}, u32[]{:S(2)}) %collective-permute-start.1) | collective-permute-done | bytes 1048608 | tf_op jit(solution)/shard_map/ppermute | solution.py:22
  92.0 2.5 collective-permute-start.3
  94.5 3.7 %collective-permute-start.2 = (bf16[64,32,256]{2,0,1:T(8,128)(2,1)}, bf16[64,32,256]{2,0,1:T(8,128)(2,1)}, u32[]{:S(2)}, u32[]{:S(2)}) collective-permute-start(bf16[64,32,256]{2,0,1:T(8,128)(2,1)} %collective-permute-done), channel_id=1, source_target_pairs={{0,28},{4,0},{8,4},{12,8},{16,12},{20,16},{24,20},{28,24},{1,29},{... | collective-permute-start | bytes 3145736 | tf_op jit(solution)/shard_map/ppermute | solution.py:24
  98.2 40.3 %collective-permute-done.3 = bf16[64,32,256]{2,0,1:T(8,128)(2,1)} collective-permute-done((bf16[64,32,256]{2,0,1:T(8,128)(2,1)S(1)}, bf16[64,32,256]{2,0,1:T(8,128)(2,1)}, u32[]{:S(2)}, u32[]{:S(2)}) %collective-permute-start.3) | collective-permute-done | bytes 1048608 | tf_op jit(solution)/shard_map/ppermute | solution.py:22
  138.5 2.6 %collective-permute-start.5 = (bf16[64,32,256]{2,0,1:T(8,128)(2,1)}, bf16[64,32,256]{2,0,1:T(8,128)(2,1)}, u32[]{:S(2)}, u32[]{:S(2)}) collective-permute-start(bf16[64,32,256]{2,0,1:T(8,128)(2,1)} %collective-permute-done.3), channel_id=1, source_target_pairs={{0,4},{4,8},{8,12},{12,16},{16,20},{20,24},{24,28},{28,0},{1,5},{5... | collective-permute-start | bytes 3145736 | tf_op jit(solution)/shard_map/ppermute | solution.py:22
  141.2 3.7 %collective-permute-start.4 = (bf16[64,32,256]{2,0,1:T(8,128)(2,1)}, bf16[64,32,256]{2,0,1:T(8,128)(2,1)}, u32[]{:S(2)}, u32[]{:S(2)}) collective-permute-start(bf16[64,32,256]{2,0,1:T(8,128)(2,1)} %collective-permute-done.2), channel_id=1, source_target_pairs={{0,28},{4,0},{8,4},{12,8},{16,12},{20,16},{24,20},{28,24},{1,29},{... | collective-permute-start | bytes 3145736 | tf_op jit(solution)/shard_map/ppermute | solution.py:24
  144.9 39.7 %collective-permute-done.5 = bf16[64,32,256]{2,0,1:T(8,128)(2,1)} collective-permute-done((bf16[64,32,256]{2,0,1:T(8,128)(2,1)}, bf16[64,32,256]{2,0,1:T(8,128)(2,1)}, u32[]{:S(2)}, u32[]{:S(2)}) %collective-permute-start.5) | collective-permute-done | bytes 1048608 | tf_op jit(solution)/shard_map/ppermute | solution.py:22
  184.6 2.5 collective-permute-start.6
  187.1 5.0 %reshape.46 = bf16[512,32,64]{2,1,0:T(8,128)(2,1)} reshape(bf16[8,2,65536]{2,1,0:T(2,128)(2,1)S(1)} %all-to-all-done) | data formatting | bytes 4194304
  192.1 6.9 %copy.35 = bf16[64,32,8,64]{0,2,3,1:T(8,128)(2,1)} copy(bf16[64,32,8,64]{0,1,3,2:T(8,128)(2,1)} %bitcast.28) | data formatting | bytes 4194304 | tf_op jit(solution)/shard_map/all_to_all | solution.py:8
  198.9 5.4 %all_to_all.34 = bf16[512,32,64]{0,2,1:T(8,128)(2,1)S(1)} reshape(bf16[8,64,32,64]{1,0,3,2:T(8,128)(2,1)} %bitcast.29) | data formatting | bytes 4194304 | tf_op jit(solution)/shard_map/all_to_all | solution.py:8
  208.7 1.8 fusion.8
  211.0 1.7 fusion.12
  214.5 2.9 %multiply_reduce_fusion = (f32[32,256]{1,0:T(8,128)S(1)}, f32[32,256]{1,0:T(8,128)S(1)}) fusion(f32[32,64]{1,0:T(8,128)S(1)} %compare_convert_fusion, bf16[64,32,256]{2,0,1:T(8,128)(2,1)} %collective-permute-done.6, bf16[512,32,64]{0,2,1:T(8,128)(2,1)S(1)} %all_to_all.34, s32[]{:T(128)S(6)} %select_n.69, f32[32,64,256]{2,1,0:T(8,128)S(1)} %fusion.2, ...), kind=kOutput, calls=%fused_computation.3 | convolution fusion | flops 73908224 | bytes 16334852 | tf_op jit(solution)/shard_map/rem,ren->emn/dot_general | solution.py:33
  219.7 6.6 %all-to-all-start.1 = ((f32[8,1,1024]{2,1,0:T(1,128)}), f32[8,1,1024]{2,1,0:T(1,128)S(1)}, u32[]{:S(2)}, u32[]{:S(2)}) async-start(f32[8,1,1024]{2,1,0:T(1,128)} %reshape.47), calls=%async_computation.1 | async-start | bytes 65536 | tf_op jit(solution)/shard_map/all_to_all | solution.py:46
  228.2 4.9 %all-to-all-done.1 = f32[8,1,1024]{2,1,0:T(1,128)S(1)} async-done(((f32[8,1,1024]{2,1,0:T(1,128)}), f32[8,1,1024]{2,1,0:T(1,128)S(1)}, u32[]{:S(2)}, u32[]{:S(2)}) %all-to-all-start.1) | async-done | bytes 32800 | tf_op jit(solution)/shard_map/all_to_all | solution.py:46
  233.1 3.3 %all-to-all-start.2 = ((f32[8,1,1024]{2,1,0:T(1,128)}), f32[8,1,1024]{2,1,0:T(1,128)S(1)}, u32[]{:S(2)}, u32[]{:S(2)}) async-start(f32[8,1,1024]{2,1,0:T(1,128)} %reshape.49), calls=%async_computation.2 | async-start | bytes 65536 | tf_op jit(solution)/shard_map/all_to_all | solution.py:47
  238.5 6.0 %psum.7 = f32[32]{0:T(128)S(1)} all-reduce(f32[32]{0:T(128)S(1)} %reduce_sum.38), channel_id=1, replica_groups=mesh['rad'=8,'ell'=4] {'ell'}, use_global_device_ids=true, to_apply=%region_4.5 | all-reduce | flops 32 | bytes 256 | tf_op jit(solution)/shard_map/psum | solution.py:53
  247.4 6.3 %pmax.7 = f32[32]{0:T(128)S(1)} all-reduce(f32[32]{0:T(128)S(1)} %reduce_max.38), channel_id=1, replica_groups=mesh['rad'=8,'ell'=4] {'ell'}, use_global_device_ids=true, to_apply=%region_9.10 | all-reduce | flops 32 | bytes 256 | tf_op jit(solution)/shard_map/pmax | solution.py:54
  (48 shorter events, 17.1 us)
Async XLA Ops:
  17.0 7.4 %copy-start = (bf16[64,32,256]{2,1,0:T(8,128)(2,1)S(1)}, bf16[64,32,256]{2,1,0:T(8,128)(2,1)}, u32[]{:S(2)}) copy-start(bf16[64,32,256]{2,1,0:T(8,128)(2,1)} %param.4) | copy-start | bytes 3145732
  17.0 170.1 %all-to-all-start = ((bf16[8,2,65536]{2,1,0:T(2,128)(2,1)}), bf16[8,2,65536]{2,1,0:T(2,128)(2,1)S(1)}, u32[]{:S(2)}, u32[]{:S(2)}) async-start(bf16[8,2,65536]{2,1,0:T(2,128)(2,1)} %reshape.45), calls=%async_computation | async-start | bytes 4194304 | tf_op jit(solution)/shard_map/all_to_all | solution.py:8
  24.4 116.7 %copy-start.3 = (s32[32]{0:T(128)S(1)}, s32[32]{0:T(128)}, u32[]{:S(2)}) copy-start(s32[32]{0:T(128)} %param.5) | copy-start | bytes 388
  25.0 67.0 %collective-permute-start.1 = (bf16[64,32,256]{2,0,1:T(8,128)(2,1)S(1)}, bf16[64,32,256]{2,0,1:T(8,128)(2,1)S(1)}, u32[]{:S(2)}, u32[]{:S(2)}) collective-permute-start(bf16[64,32,256]{2,0,1:T(8,128)(2,1)S(1)} %copy.25), channel_id=1, source_target_pairs={{0,4},{4,8},{8,12},{12,16},{16,20},{20,24},{24,28},{28,0},{1,5},{5... | collective-permute-start | bytes 3145736 | tf_op jit(solution)/shard_map/ppermute | solution.py:22
  27.1 67.4 %collective-permute-start = (bf16[64,32,256]{2,0,1:T(8,128)(2,1)S(1)}, bf16[64,32,256]{2,0,1:T(8,128)(2,1)}, u32[]{:S(2)}, u32[]{:S(2)}) collective-permute-start(bf16[64,32,256]{2,0,1:T(8,128)(2,1)S(1)} %copy.25), channel_id=1, source_target_pairs={{0,28},{4,0},{8,4},{12,8},{16,12},{20,16},{24,20},{28,24},{1,29},{... | collective-permute-start | bytes 3145736 | tf_op jit(solution)/shard_map/ppermute | solution.py:24
  92.0 2.5 copy-start.1
  92.0 46.5 %collective-permute-start.3 = (bf16[64,32,256]{2,0,1:T(8,128)(2,1)S(1)}, bf16[64,32,256]{2,0,1:T(8,128)(2,1)}, u32[]{:S(2)}, u32[]{:S(2)}) collective-permute-start(bf16[64,32,256]{2,0,1:T(8,128)(2,1)S(1)} %collective-permute-done.1), channel_id=1, source_target_pairs={{0,4},{4,8},{8,12},{12,16},{16,20},{20,24},{24,28},{28,0},{1,5},{5... | collective-permute-start | bytes 3145736 | tf_op jit(solution)/shard_map/ppermute | solution.py:22
  94.5 46.7 %collective-permute-start.2 = (bf16[64,32,256]{2,0,1:T(8,128)(2,1)}, bf16[64,32,256]{2,0,1:T(8,128)(2,1)}, u32[]{:S(2)}, u32[]{:S(2)}) collective-permute-start(bf16[64,32,256]{2,0,1:T(8,128)(2,1)} %collective-permute-done), channel_id=1, source_target_pairs={{0,28},{4,0},{8,4},{12,8},{16,12},{20,16},{24,20},{28,24},{1,29},{... | collective-permute-start | bytes 3145736 | tf_op jit(solution)/shard_map/ppermute | solution.py:24
  138.5 46.1 %collective-permute-start.5 = (bf16[64,32,256]{2,0,1:T(8,128)(2,1)}, bf16[64,32,256]{2,0,1:T(8,128)(2,1)}, u32[]{:S(2)}, u32[]{:S(2)}) collective-permute-start(bf16[64,32,256]{2,0,1:T(8,128)(2,1)} %collective-permute-done.3), channel_id=1, source_target_pairs={{0,4},{4,8},{8,12},{12,16},{16,20},{20,24},{24,28},{28,0},{1,5},{5... | collective-permute-start | bytes 3145736 | tf_op jit(solution)/shard_map/ppermute | solution.py:22
  141.2 71.6 %collective-permute-start.4 = (bf16[64,32,256]{2,0,1:T(8,128)(2,1)}, bf16[64,32,256]{2,0,1:T(8,128)(2,1)}, u32[]{:S(2)}, u32[]{:S(2)}) collective-permute-start(bf16[64,32,256]{2,0,1:T(8,128)(2,1)} %collective-permute-done.2), channel_id=1, source_target_pairs={{0,28},{4,0},{8,4},{12,8},{16,12},{20,16},{24,20},{28,24},{1,29},{... | collective-permute-start | bytes 3145736 | tf_op jit(solution)/shard_map/ppermute | solution.py:24
  184.6 29.9 %collective-permute-start.6 = (bf16[64,32,256]{2,0,1:T(8,128)(2,1)}, bf16[64,32,256]{2,0,1:T(8,128)(2,1)}, u32[]{:S(2)}, u32[]{:S(2)}) collective-permute-start(bf16[64,32,256]{2,0,1:T(8,128)(2,1)} %collective-permute-done.5), channel_id=1, source_target_pairs={{0,4},{4,8},{8,12},{12,16},{16,20},{20,24},{24,28},{28,0},{1,5},{5... | collective-permute-start | bytes 3145736 | tf_op jit(solution)/shard_map/ppermute | solution.py:22
  208.7 1.8 copy-start.2
  219.7 13.3 %all-to-all-start.1 = ((f32[8,1,1024]{2,1,0:T(1,128)}), f32[8,1,1024]{2,1,0:T(1,128)S(1)}, u32[]{:S(2)}, u32[]{:S(2)}) async-start(f32[8,1,1024]{2,1,0:T(1,128)} %reshape.47), calls=%async_computation.1 | async-start | bytes 65536 | tf_op jit(solution)/shard_map/all_to_all | solution.py:46
  233.1 12.2 %all-to-all-start.2 = ((f32[8,1,1024]{2,1,0:T(1,128)}), f32[8,1,1024]{2,1,0:T(1,128)S(1)}, u32[]{:S(2)}, u32[]{:S(2)}) async-start(f32[8,1,1024]{2,1,0:T(1,128)} %reshape.49), calls=%async_computation.2 | async-start | bytes 65536 | tf_op jit(solution)/shard_map/all_to_all | solution.py:47
